TPU v7x, 256 devices: a whole 4x4x8 slice. The times are simulated.
256 devices in a mesh: users: 32 (over x, z), rb: 8 (over y, core).
Axes of the slice: x: 4, y: 4, z: 8, core: 2. Of those that a mesh axis runs over, the one named last changes fastest.
Arguments:
- channel: bfloat16 [32768, 32, 3, 128], P('users', 'rb'), may hold values from -13 to 13
- serving: int32 [32768], P('users'), may hold values from 0 to 63, as said below
- interferers: int32 [32768, 2], P('users'), may hold values from 0 to 63, as said below
- plan: int32 [64, 32, 16], P(None, 'rb'), may hold values from 0 to 32767, as said below
- regularizer: float32 [64], P('users'), may hold values from 0.3 to 1.5
- noise_floor: float32 [64], replicated, may hold values from 0.05 to 0.5
Outputs:
- precoders: bfloat16 [64, 32, 16, 128], P('users', 'rb')
- track_metric: float32 [32768, 32], P('users', 'rb')
- entry_rate: float32 [64, 32, 16], P('users', 'rb')
Inputs may be any that keep to these rules, and one draw needn't show every extreme that they name: `serving`: each aligned block of 1024 tracks holds exactly 16 tracks served by each cell. `interferers`: A track's 2 interfering cells differ from each other and from its serving cell; each aligned block of 1024 tracks holds exactly 16 tracks with a given cell in a given column. `plan`: each entry names a track served by that cell, and the 16 tracks of a cell on one resource block differ. Take a cell group g (cells g * 2 to g * 2 + 1) and an aligned block of 4 resource blocks: at most 8 of its entries name tracks of one aligned block of 1024 tracks.
All inputs are finite; a program needn't handle non-finite values.
Results may differ from a plain program's by a relative error of at most 0.0035.
Values may be sent and summed in bfloat16 or wider, within the bound.
No kernel may reach another device: no remote copies, remote signals or barrier semaphores. Data moves between devices by JAX's collectives and lax.ppermute only.
A program may use at most 64 MiB of HBM per device.

v0:
```python
import jax
import jax.numpy as jnp
from jax import lax
from jax.sharding import PartitionSpec as P

ITERS = 12
HIGH = lax.Precision.HIGHEST


def real_form(beam_rows):
    antennas = beam_rows.shape[-1] // 2
    turned = jnp.concatenate([beam_rows[..., antennas:], -beam_rows[..., :antennas]], axis=-1)
    return jnp.concatenate([beam_rows, turned], axis=-2)


def embed_rows(channel_rows):
    antennas = channel_rows.shape[-1] // 2
    bottom_rows = jnp.concatenate(
        [-channel_rows[..., antennas:], channel_rows[..., :antennas]], axis=-1
    )
    return jnp.concatenate([channel_rows, bottom_rows], axis=-2)


def unscaled_beams(sched_rows, regularizer):
    beam_count = sched_rows.shape[-2]
    embedded = embed_rows(sched_rows)
    gram = jnp.einsum("crkd,crjd->crkj", embedded, embedded, preferred_element_type=jnp.float32)
    identity = jnp.eye(2 * beam_count, dtype=jnp.float32)
    gram = gram + regularizer[:, None, None, None] * identity
    gram_trace = jnp.trace(gram, axis1=2, axis2=3)
    start_inverse = (2.0 / gram_trace)[:, :, None, None] * identity

    def newton_step(iteration, inverse):
        product = jnp.einsum("crkj,crjl->crkl", gram, inverse, precision=HIGH)
        return 2.0 * inverse - jnp.einsum("crkj,crjl->crkl", inverse, product, precision=HIGH)

    inverse = lax.fori_loop(0, ITERS, newton_step, start_inverse)
    return jnp.einsum(
        "crkd,crkj->crjd", embedded.astype(jnp.float32), inverse[..., :beam_count], precision=HIGH
    )


def plain_regroup(channel, send_track, send_block, my_source, my_rank, groups, capacity):
    outgoing = channel[send_track, send_block, 0].reshape(groups, capacity, channel.shape[-1])
    arrived = lax.all_to_all(outgoing, "users", split_axis=0, concat_axis=0, tiled=True)
    return arrived[my_source, my_rank]


def return_denominators(denominator, send_track, send_block, my_source, my_rank, groups, capacity):
    outgoing = denominator[send_track, send_block].reshape(groups, capacity)
    arrived = lax.all_to_all(outgoing, "users", split_axis=0, concat_axis=0, tiled=True)
    return arrived[my_source, my_rank]


def track_fold(totals, grouped_rows, piece_forms, first_cell):
    piece_cells = piece_forms.shape[0]
    rows = lax.dynamic_slice_in_dim(grouped_rows, first_cell, piece_cells, axis=1)
    projected = jnp.einsum(
        "scqrd,crkd->scqrk", rows, piece_forms, preferred_element_type=jnp.float32
    )
    energy = jnp.sum(projected * projected, axis=-1)
    current = lax.dynamic_slice_in_dim(totals, first_cell, piece_cells, axis=1)
    return lax.dynamic_update_slice_in_dim(totals, current + energy, first_cell, axis=1)


def on_device(channel, serving, interferers, plan, regularizer, noise_floor):
    track_dev, rb_dev, slot_count, row_width = channel.shape
    cell_count = plan.shape[0]
    beam_count = plan.shape[2]
    cell_dev = regularizer.shape[0]
    served = track_dev // cell_count
    groups = lax.axis_size("users")
    my_group = lax.axis_index("users")
    entries = cell_dev * rb_dev * beam_count
    capacity = 2 * entries // groups
    rb_total = rb_dev * lax.axis_size("rb")
    all_entries = plan.reshape(groups, entries)
    owned_entry = all_entries // track_dev == my_group
    position = jnp.cumsum(owned_entry.astype(jnp.int32), axis=1) - 1
    position = jnp.where(owned_entry, position, capacity)
    entry_order = lax.broadcasted_iota(jnp.int32, (groups, entries), 1)
    local_track = all_entries - my_group * track_dev
    entry_block = entry_order // beam_count % rb_dev
    slot_iota = jnp.arange(capacity, dtype=jnp.int32)
    slot_match = (position[:, None, :] == slot_iota[None, :, None]).astype(jnp.int32)
    send_track = jnp.sum(slot_match * local_track[:, None, :], axis=2).reshape(-1)
    send_block = jnp.sum(slot_match * entry_block[:, None, :], axis=2).reshape(-1)
    my_entries = lax.dynamic_slice_in_dim(all_entries, my_group, 1, axis=0)[0]
    my_source = my_entries // track_dev
    source_match = (my_source[:, None] == jnp.arange(groups, dtype=jnp.int32)[None, :]).astype(
        jnp.int32
    )
    my_rank = jnp.sum((jnp.cumsum(source_match, axis=0) - 1) * source_match, axis=1)
    sched_rows = plain_regroup(
        channel, send_track, send_block, my_source, my_rank, groups, capacity
    )
    sched_rows = sched_rows.reshape(cell_dev, rb_dev, beam_count, row_width)
    vectors = unscaled_beams(sched_rows, regularizer)
    cell_power = lax.psum(jnp.sum(vectors * vectors, axis=(1, 2, 3)), "rb")
    precoders = (vectors * lax.rsqrt(cell_power / rb_total + 1e-06)[:, None, None, None]).astype(
        jnp.bfloat16
    )
    own_forms = real_form(precoders)
    heard_cells = jnp.concatenate([serving[:, None], interferers], axis=1)
    track_iota = jnp.arange(track_dev, dtype=jnp.int32)
    slot_cells = heard_cells.T
    orders = jnp.argsort(slot_cells * track_dev + track_iota[None, :], axis=1)
    ranks = jnp.argsort(orders, axis=1)
    grouped = jnp.stack(
        [channel[orders[slot_number], :, slot_number] for slot_number in range(slot_count)]
    )
    grouped_rows = grouped.reshape(slot_count, cell_count, served, rb_dev, row_width)
    zero_powers = jnp.zeros((slot_count, cell_count, served, rb_dev), jnp.float32)
    grouped_power = track_fold(
        zero_powers,
        grouped_rows,
        real_form(lax.all_gather(precoders, "users", axis=0, tiled=True)),
        jnp.int32(0),
    )
    grouped_power = grouped_power.reshape(slot_count, track_dev, rb_dev)
    track_power = jnp.stack(
        [grouped_power[slot_number][ranks[slot_number]] for slot_number in range(slot_count)],
        axis=2,
    )
    interference = track_power[:, :, 1]
    slot_number = 2
    interference = interference + track_power[:, :, slot_number]
    floor_match = (serving[:, None] == jnp.arange(cell_count, dtype=jnp.int32)[None, :]).astype(
        jnp.float32
    )
    track_floor = jnp.sum(floor_match * noise_floor[None, :], axis=1)
    denominator = interference + track_floor[:, None]
    track_metric = jnp.log2(1.0 + track_power[:, :, 0] / denominator)
    entry_denominator = return_denominators(
        denominator, send_track, send_block, my_source, my_rank, groups, capacity
    )
    crossed = jnp.einsum(
        "crkd,crjd->crkj", sched_rows, own_forms, preferred_element_type=jnp.float32
    )
    magnitude = (
        crossed[..., :beam_count] * crossed[..., :beam_count]
        + crossed[..., beam_count:] * crossed[..., beam_count:]
    )
    identity = jnp.eye(beam_count, dtype=jnp.float32)
    signal = jnp.sum(magnitude * identity, axis=-1)
    leakage = jnp.sum(magnitude * (1.0 - identity), axis=-1)
    entry_rate = jnp.log2(
        1.0 + signal / (leakage + entry_denominator.reshape(cell_dev, rb_dev, beam_count))
    )
    return (precoders, track_metric, entry_rate)


def solution(mesh):
    return jax.shard_map(
        on_device,
        mesh=mesh,
        in_specs=(
            P("users", "rb", None, None),
            P("users"),
            P("users", None),
            P(None, "rb", None),
            P("users"),
            P(),
        ),
        out_specs=(P("users", "rb", None, None), P("users", "rb"), P("users", "rb", None)),
        check_vma=False,
    )
```

profile of v0, /device:TPU:16, one launch (start us, length us, event | category | flops | bytes accessed | tf_op | source)
XLA Modules:
  0.0 197.5 jit_solution(13397811809178925806)
XLA Ops:
  10.9 2.5 %gather_fusion = bf16[256,128]{1,0:T(8,128)(2,1)} fusion(bf16[1024,4,3,128]{3,1,2,0:T(4,128)(2,1)S(1)} %copy-done, s32[256]{0:T(256)S(1)} %bitcast.88), kind=kCustom, calls=%fused_computation | custom fusion | bytes 134144 | tf_op jit(solution)/shard_map/gather | solution.py:44
  13.4 11.3 %all-to-all-start = ((bf16[32,8,128]{2,1,0:T(8,128)(2,1)}), bf16[32,8,128]{2,1,0:T(8,128)(2,1)S(1)}, u32[]{:S(2)}, u32[]{:S(2)}) async-start(bf16[32,8,128]{2,1,0:T(8,128)(2,1)} %bitcast.2), calls=%async_computation | async-start | bytes 131072 | tf_op jit(solution)/shard_map/all_to_all | solution.py:45
  24.8 1.3 fusion.24
  28.1 7.0 %sort.34.cloned.1.call-done = (s32[3,1024]{1,0:T(4,128)}, s32[3,1024]{1,0:T(4,128)}) async-done(((s32[3,1024]{1,0:T(4,128)}, s32[3,1024]{1,0:T(4,128)}), (s32[3,1024]{1,0:T(4,128)}, s32[3,1024]{1,0:T(4,128)})) %sort.34.cloned.1.call-update) | async-done | bytes 24592 | tf_op jit(solution)/shard_map/jit(argsort)/sort | solution.py:107
  37.4 7.6 %while.10 = (s32[]{:T(128)}, f32[2,4,32,32]{2,3,1,0:T(8,128)S(1)}, f32[2,4,32,32]{3,2,1,0:T(8,128)S(1)}, s32[]{:T(128)}) while((s32[]{:T(128)}, f32[2,4,32,32]{2,3,1,0:T(8,128)S(1)}, f32[2,4,32,32]{3,2,1,0:T(8,128)S(1)}, s32[]{:T(128)}) %tuple.44), condition=%wide.region_7.8_spmd, body=%wide.region_6.7_spmd.sunk | while | flops 6307842 | bytes 262197 | solution.py:37
  45.4 10.1 %psum.7 = f32[2]{0:T(128)S(1)} all-reduce(f32[2]{0:T(128)S(1)} %get-tuple-element.71), channel_id=1, replica_groups=mesh['users'=32,'rb'=8] {'rb'}, use_global_device_ids=true, to_apply=%region_9.10 | all-reduce | flops 2 | bytes 16 | tf_op jit(solution)/shard_map/psum | solution.py:99
  57.8 8.9 %gather_fusion.3 = bf16[1024,4,128]{2,1,0:T(4,128)(2,1)} fusion(bf16[1024,4,3,128]{3,1,2,0:T(4,128)(2,1)S(1)} %copy-done, s32[1024]{0:T(1024)S(1)} %bitcast.87), kind=kCustom, calls=%fused_computation.3 | custom fusion | bytes 2105344 | tf_op jit(solution)/shard_map/gather | solution.py:110
  66.6 2.5 %copy.57 = bf16[1,64,16,4,128]{4,2,0,3,1:T(8,128)(2,1)} copy(bf16[1,64,16,4,128]{4,3,2,1,0:T(4,128)(2,1)} %bitcast.94) | data formatting | bytes 2097152 | tf_op jit(solution)/shard_map/stack | solution.py:109
  69.2 8.9 %gather_fusion.4 = bf16[1024,4,128]{2,1,0:T(4,128)(2,1)} fusion(bf16[1024,4,3,128]{3,1,2,0:T(4,128)(2,1)S(1)} %copy-done, s32[1024]{0:T(1024)S(1)} %bitcast.86), kind=kCustom, calls=%fused_computation.4 | custom fusion | bytes 2105344 | tf_op jit(solution)/shard_map/gather | solution.py:110
  78.0 2.5 %copy.58 = bf16[1,64,16,4,128]{4,2,0,3,1:T(8,128)(2,1)} copy(bf16[1,64,16,4,128]{4,3,2,1,0:T(4,128)(2,1)} %bitcast.95) | data formatting | bytes 2097152 | tf_op jit(solution)/shard_map/stack | solution.py:109
  80.5 8.9 %gather_fusion.2 = bf16[1024,4,128]{2,1,0:T(4,128)(2,1)} fusion(bf16[1024,4,3,128]{3,1,2,0:T(4,128)(2,1)S(1)} %copy-done, s32[1024]{0:T(1024)S(1)} %bitcast.85), kind=kCustom, calls=%fused_computation.2 | custom fusion | bytes 2105344 | tf_op jit(solution)/shard_map/gather | solution.py:110
  89.4 2.5 %copy.56 = bf16[1,64,16,4,128]{4,2,0,3,1:T(8,128)(2,1)} copy(bf16[1,64,16,4,128]{4,3,2,1,0:T(4,128)(2,1)} %bitcast.96) | data formatting | bytes 2097152 | tf_op jit(solution)/shard_map/stack | solution.py:109
  93.0 42.4 %all-gather.2.cloned.1.call-done = bf16[64,4,16,128]{3,2,1,0:T(8,128)(2,1)} async-done(((bf16[2,4,16,128]{3,2,1,0:T(8,128)(2,1)}), bf16[64,4,16,128]{3,2,1,0:T(8,128)(2,1)}) %all-gather.2.cloned.1.call-update) | async-done | bytes 1048592 | tf_op jit(solution)/shard_map/all_gather | solution.py:117
  135.4 2.1 %fusion.53 = (bf16[64,4,16,64]{3,2,1,0:T(8,128)(2,1)S(1)}, bf16[64,4,16,64]{3,2,1,0:T(8,128)(2,1)S(1)}) fusion(bf16[64,4,16,128]{3,2,1,0:T(8,128)(2,1)} %all-gather.2.cloned.1.call-done), kind=kLoop, calls=%fused_computation.137 | loop fusion | flops 262144 | bytes 2097152 | tf_op jit(solution)/shard_map/slice | solution.py:12
  138.2 2.7 %multiply_reduce_fusion = f32[64,4,3,16]{3,2,1,0:T(4,128)S(1)} fusion(bf16[1,64,16,4,128]{4,2,0,3,1:T(8,128)(2,1)S(1)} %copy-done.3, bf16[1,64,16,4,128]{4,2,0,3,1:T(8,128)(2,1)S(1)} %copy-done.2, bf16[1,64,16,4,128]{4,2,0,3,1:T(8,128)(2,1)S(1)} %copy-done.4, bf16[64,4,16,64]{3,2,1,0:T(8,128)(2,1)S(1)} %get-tuple-element.55, ...), kind=kOutput, calls=%fused_computation.12 | convolution fusion | flops 117166080 | bytes 5292032 | tf_op jit(solution)/shard_map/scqrd,crkd->scqrk/dot_general | solution.py:58
  141.9 2.2 %copy.61 = f32[1,64,16,4]{3,2,1,0:T(8,128)} copy(f32[1,64,16,4]{2,0,3,1:T(1,128)} %get-tuple-element.56) | data formatting | bytes 32768 | tf_op jit(solution)/shard_map/slice | solution.py:122
  146.5 5.0 %gather_fusion.7 = f32[1024,4]{1,0:T(8,128)} fusion(f32[1024,4]{1,0:T(8,128)} %bitcast.92, s32[1024]{0:T(1024)S(1)} %broadcast_clamp_fusion), kind=kCustom, calls=%fused_computation.7 | custom fusion | bytes 36864 | tf_op jit(solution)/shard_map/gather | solution.py:122
  151.6 5.0 %gather_fusion.6 = f32[1024,4]{1,0:T(8,128)} fusion(f32[1024,4]{1,0:T(8,128)} %bitcast.90, s32[1024]{0:T(1024)S(1)} %broadcast_clamp_fusion.1), kind=kCustom, calls=%fused_computation.6 | custom fusion | bytes 36864 | tf_op jit(solution)/shard_map/gather | solution.py:122
  156.6 5.0 %gather_fusion.5 = f32[1024,4]{1,0:T(8,128)} fusion(f32[1024,4]{1,0:T(8,128)} %bitcast.91, s32[1024]{0:T(1024)S(1)} %broadcast_clamp_fusion.2), kind=kCustom, calls=%fused_computation.5 | custom fusion | bytes 36864 | tf_op jit(solution)/shard_map/gather | solution.py:122
  161.6 2.6 %log_multiply_fusion = (f32[1024,4]{1,0:T(8,128)}, f32[1024,4]{1,0:T(8,128)}) fusion(f32[1024,4]{1,0:T(8,128)} %gather_fusion.5, f32[1024]{0:T(1024)S(1)} %select_reduce_fusion, f32[1024,4]{1,0:T(8,128)} %gather_fusion.6, f32[1024,4]{1,0:T(8,128)} %gather_fusion.7), kind=kLoop, calls=%fused_computation.25 | loop fusion | flops 20480 | bytes 86016 | tf_op jit(solution)/shard_map/log2 | solution.py:133
  164.2 5.6 %gather_fusion.8 = f32[256]{0:T(256)S(1)} fusion(f32[1024,4]{1,0:T(8,128)} %get-tuple-element.51, s32[256]{0:T(256)S(1)} %bitcast.89), kind=kCustom, calls=%fused_computation.8 | custom fusion | bytes 4096 | tf_op jit(solution)/shard_map/gather | solution.py:50
  170.5 7.8 %all-to-all-start.1 = ((f32[32,1,8]{2,1,0:T(1,128)}), f32[32,1,8]{2,1,0:T(1,128)S(1)}, u32[]{:S(2)}, u32[]{:S(2)}) async-start(f32[32,1,8]{2,1,0:T(1,128)} %bitcast.31), calls=%async_computation.1 | async-start | bytes 32768 | tf_op jit(solution)/shard_map/all_to_all | solution.py:51
  178.5 1.8 copy.63
  180.4 7.8 %all-to-all-done.1 = f32[32,1,8]{2,1,0:T(1,128)S(1)} async-done(((f32[32,1,8]{2,1,0:T(1,128)}), f32[32,1,8]{2,1,0:T(1,128)S(1)}, u32[]{:S(2)}, u32[]{:S(2)}) %all-to-all-start.1) | async-done | bytes 1056 | tf_op jit(solution)/shard_map/all_to_all | solution.py:51
  (109 shorter events, 24.9 us)
Async XLA Ops:
  8.0 2.9 %copy-start = (bf16[1024,4,3,128]{3,1,2,0:T(4,128)(2,1)S(1)}, bf16[1024,4,3,128]{3,1,2,0:T(4,128)(2,1)}, u32[]{:S(2)}) copy-start(bf16[1024,4,3,128]{3,1,2,0:T(4,128)(2,1)} %param.8) | copy-start | bytes 9437188
  13.4 22.4 %all-to-all-start = ((bf16[32,8,128]{2,1,0:T(8,128)(2,1)}), bf16[32,8,128]{2,1,0:T(8,128)(2,1)S(1)}, u32[]{:S(2)}, u32[]{:S(2)}) async-start(bf16[32,8,128]{2,1,0:T(8,128)(2,1)} %bitcast.2), calls=%async_computation | async-start | bytes 131072 | tf_op jit(solution)/shard_map/all_to_all | solution.py:45
  24.8 10.4 %sort.34.cloned.1.call-start = ((), (), s32[]{:S(2)}) async-start(), calls=%async_computation.3 | async-start | bytes 98336 | tf_op jit(solution)/shard_map/jit(argsort)/sort | solution.py:107
  26.8 65.1 %sort.36.cloned.1.call-start = ((), (), s32[]{:S(2)}) async-start(), calls=%async_computation.4 | async-start | bytes 98336 | tf_op jit(solution)/shard_map/jit(argsort)/sort | solution.py:108
  35.8 99.7 %all-gather.2.cloned.1.call-start = ((), (), s32[]{:S(2)}) async-start(), calls=%async_computation.2 | async-start | bytes 1081344 | tf_op jit(solution)/shard_map/all_gather | solution.py:117
  37.0 20.7 %copy-start.6 = (s32[3,1024]{1,0:T(4,128)S(1)}, s32[3,1024]{1,0:T(4,128)}, u32[]{:S(2)}) copy-start(s32[3,1024]{1,0:T(4,128)} %get-tuple-element.23) | copy-start | bytes 36868
  78.0 14.7 %copy-start.5 = (bf16[2,4,16,128]{3,2,1,0:T(8,128)(2,1)S(1)}, bf16[2,4,16,128]{3,2,1,0:T(8,128)(2,1)}, u32[]{:S(2)}) copy-start(bf16[2,4,16,128]{3,2,1,0:T(8,128)(2,1)} %multiply_convert_fusion) | copy-start | bytes 98308
  135.4 2.1 %copy-start.1 = (bf16[64,4,16,128]{3,2,1,0:T(8,128)(2,1)S(1)}, bf16[64,4,16,128]{3,2,1,0:T(8,128)(2,1)}, u32[]{:S(2)}) copy-start(bf16[64,4,16,128]{3,2,1,0:T(8,128)(2,1)} %all-gather.2.cloned.1.call-done) | copy-start | bytes 3145732
  135.4 2.2 %copy-start.2 = (bf16[1,64,16,4,128]{4,2,0,3,1:T(8,128)(2,1)S(1)}, bf16[1,64,16,4,128]{4,2,0,3,1:T(8,128)(2,1)}, u32[]{:S(2)}) copy-start(bf16[1,64,16,4,128]{4,2,0,3,1:T(8,128)(2,1)} %copy.57) | copy-start | bytes 3145732
  135.4 2.5 %copy-start.3 = (bf16[1,64,16,4,128]{4,2,0,3,1:T(8,128)(2,1)S(1)}, bf16[1,64,16,4,128]{4,2,0,3,1:T(8,128)(2,1)}, u32[]{:S(2)}) copy-start(bf16[1,64,16,4,128]{4,2,0,3,1:T(8,128)(2,1)} %copy.58) | copy-start | bytes 3145732
  135.4 2.8 %copy-start.4 = (bf16[1,64,16,4,128]{4,2,0,3,1:T(8,128)(2,1)S(1)}, bf16[1,64,16,4,128]{4,2,0,3,1:T(8,128)(2,1)}, u32[]{:S(2)}) copy-start(bf16[1,64,16,4,128]{4,2,0,3,1:T(8,128)(2,1)} %copy.56) | copy-start | bytes 3145732
  156.6 21.7 %copy-start.7 = (f32[16,16]{1,0:T(8,128)S(1)}, f32[16,16]{1,0:T(8,128)}, u32[]{:S(2)}) copy-start(f32[16,16]{1,0:T(8,128)} %fusion.26) | copy-start | bytes 3076
  170.5 17.7 %all-to-all-start.1 = ((f32[32,1,8]{2,1,0:T(1,128)}), f32[32,1,8]{2,1,0:T(1,128)S(1)}, u32[]{:S(2)}, u32[]{:S(2)}) async-start(f32[32,1,8]{2,1,0:T(1,128)} %bitcast.31), calls=%async_computation.1 | async-start | bytes 32768 | tf_op jit(solution)/shard_map/all_to_all | solution.py:51
Sparse Core Ops, SparseCore 0:
  28.6 6.2 sort.38.cloned.1.call-done
  38.2 4.3 sort.40.cloned.1.call-done
  (2 shorter events, 0.0 us)
Sparse Core Ops, SparseCore 1:
  56.4 79.0 all-gather.1
where the time goes:
time: 199 us; the launch traced here: 198 us
  local copies, waits for them, and re-layouts  78.3 us (39%)
  waiting for transfers between devices  50.2 us (25%)
  starting transfers between devices  19.2 us (10%)
  between operations  15.8 us (8%)
  other arithmetic  12.8 us (6%)
  matrix products  10.6 us (5%)
  blocking collectives  10.1 us (5%)
    all_gather x1, waiting for transfers between devices, on_device(): lax.all_gather(precoders, 'users', axis=0, tiled=True)  42.4 us
    gather x3, local copies, waits for them, and re-layouts, on_device(): channel[orders[slot_number], :, slot_number]  26.6 us
    gather x3, local copies, waits for them, and re-layouts, on_device(): grouped_power[slot_number][ranks[slot_number]]  15.1 us
    all_to_all x1, starting transfers between devices, plain_regroup(): lax.all_to_all(outgoing, 'users', split_axis=0, concat_axis=0, tiled=True)  11.3 us
    psum x1, blocking collectives, on_device(): cell_power = lax.psum(jnp.sum(vectors * vectors, axis=(1, 2, 3)), 'rb')  10.1 us
    all_to_all x1, starting transfers between devices, return_denominators(): lax.all_to_all(outgoing, 'users', split_axis=0, concat_axis=0, tiled=True)  7.84 us
    all_to_all x1, waiting for transfers between devices, return_denominators(): lax.all_to_all(outgoing, 'users', split_axis=0, concat_axis=0, tiled=True)  7.76 us
    another operation x3, local copies, waits for them, and re-layouts, on_device(): jnp.stack([channel[orders[slot_number], :, slot_number] for slot_number i...  7.47 us
  transfers between devices with their start and end apart: 3, of which 2 were waited for; matrix products, arithmetic and copies ran while one was open for 22% of the time, Pallas kernels for 0%

commit v1 on v0

--- a/solution.py
+++ b/solution.py
@@ -5,6 +5,13 @@
 
 ITERS = 12
 HIGH = lax.Precision.HIGHEST
+
+
+def gather_over(x, axis, dim):
+    count = lax.axis_size(axis)
+    blocks = jnp.stack([x for _ in range(count)])
+    blocks = lax.all_to_all(blocks, axis, split_axis=0, concat_axis=0)
+    return jnp.concatenate(blocks, axis=dim)
 
 
 def real_form(beam_rows):
@@ -112,10 +119,7 @@
     grouped_rows = grouped.reshape(slot_count, cell_count, served, rb_dev, row_width)
     zero_powers = jnp.zeros((slot_count, cell_count, served, rb_dev), jnp.float32)
     grouped_power = track_fold(
-        zero_powers,
-        grouped_rows,
-        real_form(lax.all_gather(precoders, "users", axis=0, tiled=True)),
-        jnp.int32(0),
+        zero_powers, grouped_rows, real_form(gather_over(precoders, "users", 0)), jnp.int32(0)
     )
     grouped_power = grouped_power.reshape(slot_count, track_dev, rb_dev)
     track_power = jnp.stack(

time: 199 us -> 175 us (0.88)
  waiting for transfers between devices: 50.2 us -> 16.5 us
  starting transfers between devices: 19.2 us -> 26.6 us
  local copies, waits for them, and re-layouts: 78.3 us -> 81.1 us
    all_gather x1 -> x0, waiting for transfers between devices: 42.4 us -> none  [on_device(): lax.all_gather(precoders, 'users', axis=0, tiled=True)]
    all_to_all x1, waiting for transfers between devices: 0.01 us -> 8.7 us  [plain_regroup(): lax.all_to_all(outgoing, 'users', split_axis=0, concat_axis=0, tiled=True)]
    all_to_all x0 -> x1, starting transfers between devices: none -> 4.66 us  [gather_over(): blocks = lax.all_to_all(blocks, axis, split_axis=0, concat_axis=0)]
    all_to_all x1, starting transfers between devices: 7.84 us -> 10.7 us  [return_denominators(): lax.all_to_all(outgoing, 'users', split_axis=0, concat_axis=0, tiled=True)]
  transfers between devices with their start and end apart: 3 -> 3, of which waited for: 2 -> 2; matrix products, arithmetic and copies ran while one was open for 22% -> 24% of each run, Pallas kernels for 0% -> 0%
where the time goes in v1:
time: 175 us; the launch traced here: 172 us
  local copies, waits for them, and re-layouts  81.1 us (46%)
  starting transfers between devices  26.6 us (15%)
  waiting for transfers between devices  16.5 us (9%)
  between operations  14.4 us (8%)
  matrix products  11.4 us (7%)
  other arithmetic  11 us (6%)
  blocking collectives  10.4 us (6%)
    gather x3, local copies, waits for them, and re-layouts, on_device(): channel[orders[slot_number], :, slot_number]  26.6 us
    gather x3, local copies, waits for them, and re-layouts, on_device(): grouped_power[slot_number][ranks[slot_number]]  15.1 us
    all_to_all x1, starting transfers between devices, plain_regroup(): lax.all_to_all(outgoing, 'users', split_axis=0, concat_axis=0, tiled=True)  11.3 us
    all_to_all x1, starting transfers between devices, return_denominators(): lax.all_to_all(outgoing, 'users', split_axis=0, concat_axis=0, tiled=True)  10.7 us
    psum x1, blocking collectives, on_device(): cell_power = lax.psum(jnp.sum(vectors * vectors, axis=(1, 2, 3)), 'rb')  10.4 us
    sort x2, local copies, waits for them, and re-layouts, on_device(): orders = jnp.argsort(slot_cells * track_dev + track_iota[None, :], axis=1)  8.7 us
    all_to_all x1, waiting for transfers between devices, plain_regroup(): lax.all_to_all(outgoing, 'users', split_axis=0, concat_axis=0, tiled=True)  8.7 us
    all_to_all x1, waiting for transfers between devices, return_denominators(): lax.all_to_all(outgoing, 'users', split_axis=0, concat_axis=0, tiled=True)  7.78 us
  transfers between devices with their start and end apart: 3, of which 2 were waited for; matrix products, arithmetic and copies ran while one was open for 24% of the time, Pallas kernels for 0%

profile of v1, /device:TPU:16, one launch (start us, length us, event | category | flops | bytes accessed | tf_op | source)
XLA Modules:
  0.0 171.9 jit_solution(500374873413706323)
XLA Ops:
  10.1 2.5 %gather_fusion = bf16[256,128]{1,0:T(8,128)(2,1)} fusion(bf16[1024,4,3,128]{3,1,2,0:T(4,128)(2,1)S(1)} %copy-done, s32[256]{0:T(256)S(1)} %bitcast.89), kind=kCustom, calls=%fused_computation | custom fusion | bytes 134144 | tf_op jit(solution)/shard_map/gather | solution.py:51
  12.6 11.3 %all-to-all-start = ((bf16[32,8,128]{2,1,0:T(8,128)(2,1)}), bf16[32,8,128]{2,1,0:T(8,128)(2,1)S(1)}, u32[]{:S(2)}, u32[]{:S(2)}) async-start(bf16[32,8,128]{2,1,0:T(8,128)(2,1)} %bitcast.2), calls=%async_computation | async-start | bytes 131072 | tf_op jit(solution)/shard_map/all_to_all | solution.py:52
  25.2 8.7 %all-to-all-done = bf16[32,8,128]{2,1,0:T(8,128)(2,1)S(1)} async-done(((bf16[32,8,128]{2,1,0:T(8,128)(2,1)}), bf16[32,8,128]{2,1,0:T(8,128)(2,1)S(1)}, u32[]{:S(2)}, u32[]{:S(2)}) %all-to-all-start) | async-done | bytes 65568 | tf_op jit(solution)/shard_map/all_to_all | solution.py:52
  35.6 7.6 %while.10 = (s32[]{:T(128)}, f32[2,4,32,32]{2,3,1,0:T(8,128)S(1)}, f32[2,4,32,32]{3,2,1,0:T(8,128)S(1)}, s32[]{:T(128)}) while((s32[]{:T(128)}, f32[2,4,32,32]{2,3,1,0:T(8,128)S(1)}, f32[2,4,32,32]{3,2,1,0:T(8,128)S(1)}, s32[]{:T(128)}) %tuple.44), condition=%wide.region_7.8_spmd, body=%wide.region_6.7_spmd.sunk | while | flops 6307842 | bytes 262197 | solution.py:44
  43.6 10.4 %psum.7 = f32[2]{0:T(128)S(1)} all-reduce(f32[2]{0:T(128)S(1)} %get-tuple-element.71), channel_id=1, replica_groups=mesh['users'=32,'rb'=8] {'rb'}, use_global_device_ids=true, to_apply=%region_9.10 | all-reduce | flops 2 | bytes 16 | tf_op jit(solution)/shard_map/psum | solution.py:106
  55.4 4.7 %all-to-all-start.1 = ((bf16[32,2,4,16,128]{4,3,2,1,0:T(8,128)(2,1)}), bf16[32,2,4,16,128]{4,3,2,1,0:T(8,128)(2,1)}, u32[]{:S(2)}, u32[]{:S(2)}) async-start(bf16[32,2,4,16,128]{4,3,2,1,0:T(8,128)(2,1)} %stack.10), calls=%async_computation.1 | async-start | bytes 2097152 | tf_op jit(solution)/shard_map/all_to_all | solution.py:13
  61.7 8.7 %sort.34.cloned.1.call-done = (s32[3,1024]{1,0:T(4,128)}, s32[3,1024]{1,0:T(4,128)}) async-done(((s32[3,1024]{1,0:T(4,128)}, s32[3,1024]{1,0:T(4,128)}), (s32[3,1024]{1,0:T(4,128)}, s32[3,1024]{1,0:T(4,128)})) %sort.34.cloned.1.call-update) | async-done | bytes 24592 | tf_op jit(solution)/shard_map/jit(argsort)/sort | solution.py:114
  71.9 8.9 %gather_fusion.3 = bf16[1024,4,128]{2,1,0:T(4,128)(2,1)} fusion(bf16[1024,4,3,128]{3,1,2,0:T(4,128)(2,1)S(1)} %copy-done, s32[1024]{0:T(1024)S(1)} %bitcast.88), kind=kCustom, calls=%fused_computation.3 | custom fusion | bytes 2105344 | tf_op jit(solution)/shard_map/gather | solution.py:117
  80.8 2.5 %copy.57 = bf16[1,64,16,4,128]{4,2,0,3,1:T(8,128)(2,1)} copy(bf16[1,64,16,4,128]{4,3,2,1,0:T(4,128)(2,1)} %bitcast.95) | data formatting | bytes 2097152 | tf_op jit(solution)/shard_map/stack | solution.py:116
  83.2 8.9 %gather_fusion.4 = bf16[1024,4,128]{2,1,0:T(4,128)(2,1)} fusion(bf16[1024,4,3,128]{3,1,2,0:T(4,128)(2,1)S(1)} %copy-done, s32[1024]{0:T(1024)S(1)} %bitcast.87), kind=kCustom, calls=%fused_computation.4 | custom fusion | bytes 2105344 | tf_op jit(solution)/shard_map/gather | solution.py:117
  92.1 2.5 %copy.58 = bf16[1,64,16,4,128]{4,2,0,3,1:T(8,128)(2,1)} copy(bf16[1,64,16,4,128]{4,3,2,1,0:T(4,128)(2,1)} %bitcast.96) | data formatting | bytes 2097152 | tf_op jit(solution)/shard_map/stack | solution.py:116
  94.6 8.9 %gather_fusion.2 = bf16[1024,4,128]{2,1,0:T(4,128)(2,1)} fusion(bf16[1024,4,3,128]{3,1,2,0:T(4,128)(2,1)S(1)} %copy-done, s32[1024]{0:T(1024)S(1)} %bitcast.86), kind=kCustom, calls=%fused_computation.2 | custom fusion | bytes 2105344 | tf_op jit(solution)/shard_map/gather | solution.py:117
  103.5 2.5 %copy.56 = bf16[1,64,16,4,128]{4,2,0,3,1:T(8,128)(2,1)} copy(bf16[1,64,16,4,128]{4,3,2,1,0:T(4,128)(2,1)} %bitcast.97) | data formatting | bytes 2097152 | tf_op jit(solution)/shard_map/stack | solution.py:116
  107.2 2.1 %fusion.53 = (bf16[64,4,16,64]{3,2,1,0:T(8,128)(2,1)S(1)}, bf16[64,4,16,64]{3,2,1,0:T(8,128)(2,1)S(1)}) fusion(bf16[64,4,16,128]{3,2,1,0:T(8,128)(2,1)} %bitcast.8), kind=kLoop, calls=%fused_computation.137 | loop fusion | flops 262144 | bytes 2097152 | tf_op jit(solution)/shard_map/slice | solution.py:19
  109.6 3.5 %multiply_reduce_fusion = f32[64,4,3,16]{3,2,1,0:T(4,128)S(1)} fusion(bf16[1,64,16,4,128]{4,2,0,3,1:T(8,128)(2,1)S(1)} %copy-done.2, bf16[1,64,16,4,128]{4,2,0,3,1:T(8,128)(2,1)S(1)} %copy-done.1, bf16[1,64,16,4,128]{4,2,0,3,1:T(8,128)(2,1)S(1)} %copy-done.3, bf16[64,4,16,64]{3,2,1,0:T(8,128)(2,1)S(1)} %get-tuple-element.55, ...), kind=kOutput, calls=%fused_computation.12 | convolution fusion | flops 117166080 | bytes 5292032 | tf_op jit(solution)/shard_map/scqrd,crkd->scqrk/dot_general | solution.py:65
  114.1 2.2 %copy.61 = f32[1,64,16,4]{3,2,1,0:T(8,128)} copy(f32[1,64,16,4]{2,0,3,1:T(1,128)} %get-tuple-element.56) | data formatting | bytes 32768 | tf_op jit(solution)/shard_map/slice | solution.py:126
  118.7 5.0 %gather_fusion.7 = f32[1024,4]{1,0:T(8,128)} fusion(f32[1024,4]{1,0:T(8,128)} %bitcast.93, s32[1024]{0:T(1024)S(1)} %broadcast_clamp_fusion), kind=kCustom, calls=%fused_computation.7 | custom fusion | bytes 36864 | tf_op jit(solution)/shard_map/gather | solution.py:126
  123.8 5.0 %gather_fusion.6 = f32[1024,4]{1,0:T(8,128)} fusion(f32[1024,4]{1,0:T(8,128)} %bitcast.91, s32[1024]{0:T(1024)S(1)} %broadcast_clamp_fusion.1), kind=kCustom, calls=%fused_computation.6 | custom fusion | bytes 36864 | tf_op jit(solution)/shard_map/gather | solution.py:126
  128.8 5.0 %gather_fusion.5 = f32[1024,4]{1,0:T(8,128)} fusion(f32[1024,4]{1,0:T(8,128)} %bitcast.92, s32[1024]{0:T(1024)S(1)} %broadcast_clamp_fusion.2), kind=kCustom, calls=%fused_computation.5 | custom fusion | bytes 36864 | tf_op jit(solution)/shard_map/gather | solution.py:126
  133.8 2.6 %log_multiply_fusion = (f32[1024,4]{1,0:T(8,128)}, f32[1024,4]{1,0:T(8,128)}) fusion(f32[1024,4]{1,0:T(8,128)} %gather_fusion.5, f32[1024]{0:T(1024)S(1)} %select_reduce_fusion, f32[1024,4]{1,0:T(8,128)} %gather_fusion.6, f32[1024,4]{1,0:T(8,128)} %gather_fusion.7), kind=kLoop, calls=%fused_computation.25 | loop fusion | flops 20480 | bytes 86016 | tf_op jit(solution)/shard_map/log2 | solution.py:137
  136.4 5.6 %gather_fusion.8 = f32[256]{0:T(256)S(1)} fusion(f32[1024,4]{1,0:T(8,128)} %get-tuple-element.51, s32[256]{0:T(256)S(1)} %bitcast.90), kind=kCustom, calls=%fused_computation.8 | custom fusion | bytes 4096 | tf_op jit(solution)/shard_map/gather | solution.py:57
  142.6 10.7 %all-to-all-start.2 = ((f32[32,1,8]{2,1,0:T(1,128)}), f32[32,1,8]{2,1,0:T(1,128)S(1)}, u32[]{:S(2)}, u32[]{:S(2)}) async-start(f32[32,1,8]{2,1,0:T(1,128)} %bitcast.32), calls=%async_computation.2 | async-start | bytes 32768 | tf_op jit(solution)/shard_map/all_to_all | solution.py:58
  153.5 1.8 %copy.63 = f32[1024,4]{0,1:T(4,128)} copy(f32[1024,4]{1,0:T(8,128)} %get-tuple-element.50) | data formatting | bytes 32768
  155.3 7.8 %all-to-all-done.2 = f32[32,1,8]{2,1,0:T(1,128)S(1)} async-done(((f32[32,1,8]{2,1,0:T(1,128)}), f32[32,1,8]{2,1,0:T(1,128)S(1)}, u32[]{:S(2)}, u32[]{:S(2)}) %all-to-all-start.2) | async-done | bytes 1056 | tf_op jit(solution)/shard_map/all_to_all | solution.py:58
  (109 shorter events, 25.5 us)
Async XLA Ops:
  7.2 2.9 %copy-start = (bf16[1024,4,3,128]{3,1,2,0:T(4,128)(2,1)S(1)}, bf16[1024,4,3,128]{3,1,2,0:T(4,128)(2,1)}, u32[]{:S(2)}) copy-start(bf16[1024,4,3,128]{3,1,2,0:T(4,128)(2,1)} %param.8) | copy-start | bytes 9437188
  12.6 21.3 %all-to-all-start = ((bf16[32,8,128]{2,1,0:T(8,128)(2,1)}), bf16[32,8,128]{2,1,0:T(8,128)(2,1)S(1)}, u32[]{:S(2)}, u32[]{:S(2)}) async-start(bf16[32,8,128]{2,1,0:T(8,128)(2,1)} %bitcast.2), calls=%async_computation | async-start | bytes 131072 | tf_op jit(solution)/shard_map/all_to_all | solution.py:52
  35.6 24.5 %copy-start.5 = (s32[1024]{0:T(1024)S(1)}, s32[1024]{0:T(1024)}, u32[]{:S(2)}) copy-start(s32[1024]{0:T(1024)} %param.9) | copy-start | bytes 12292
  35.6 24.5 %copy-start.6 = (s32[1024,2]{0,1:T(2,128)S(1)}, s32[1024,2]{0,1:T(2,128)}, u32[]{:S(2)}) copy-start(s32[1024,2]{0,1:T(2,128)} %param.10) | copy-start | bytes 24580
  35.6 26.0 %copy-start.7 = (f32[64]{0:T(128)S(1)}, f32[64]{0:T(128)}, u32[]{:S(2)}) copy-start(f32[64]{0:T(128)} %param.13) | copy-start | bytes 772
  54.1 52.8 %copy-start.4 = (bf16[2,4,16,128]{3,2,1,0:T(8,128)(2,1)}, bf16[2,4,16,128]{3,2,1,0:T(8,128)(2,1)S(1)}, u32[]{:S(2)}) copy-start(bf16[2,4,16,128]{3,2,1,0:T(8,128)(2,1)S(1)} %multiply_convert_fusion) | copy-start | bytes 98308
  55.4 51.8 %all-to-all-start.1 = ((bf16[32,2,4,16,128]{4,3,2,1,0:T(8,128)(2,1)}), bf16[32,2,4,16,128]{4,3,2,1,0:T(8,128)(2,1)}, u32[]{:S(2)}, u32[]{:S(2)}) async-start(bf16[32,2,4,16,128]{4,3,2,1,0:T(8,128)(2,1)} %stack.10), calls=%async_computation.1 | async-start | bytes 2097152 | tf_op jit(solution)/shard_map/all_to_all | solution.py:13
  60.0 10.4 %sort.34.cloned.1.call-start = ((), (), s32[]{:S(2)}) async-start(), calls=%async_computation.3 | async-start | bytes 98336 | tf_op jit(solution)/shard_map/jit(argsort)/sort | solution.py:114
  61.4 44.6 %sort.36.cloned.1.call-start = ((), (), s32[]{:S(2)}) async-start(), calls=%async_computation.4 | async-start | bytes 98336 | tf_op jit(solution)/shard_map/jit(argsort)/sort | solution.py:115
  107.2 2.1 %copy-start.1 = (bf16[1,64,16,4,128]{4,2,0,3,1:T(8,128)(2,1)S(1)}, bf16[1,64,16,4,128]{4,2,0,3,1:T(8,128)(2,1)}, u32[]{:S(2)}) copy-start(bf16[1,64,16,4,128]{4,2,0,3,1:T(8,128)(2,1)} %copy.57) | copy-start | bytes 3145732
  107.2 2.2 %copy-start.2 = (bf16[1,64,16,4,128]{4,2,0,3,1:T(8,128)(2,1)S(1)}, bf16[1,64,16,4,128]{4,2,0,3,1:T(8,128)(2,1)}, u32[]{:S(2)}) copy-start(bf16[1,64,16,4,128]{4,2,0,3,1:T(8,128)(2,1)} %copy.58) | copy-start | bytes 3145732
  107.2 2.5 %copy-start.3 = (bf16[1,64,16,4,128]{4,2,0,3,1:T(8,128)(2,1)S(1)}, bf16[1,64,16,4,128]{4,2,0,3,1:T(8,128)(2,1)}, u32[]{:S(2)}) copy-start(bf16[1,64,16,4,128]{4,2,0,3,1:T(8,128)(2,1)} %copy.56) | copy-start | bytes 3145732
  142.6 20.5 %all-to-all-start.2 = ((f32[32,1,8]{2,1,0:T(1,128)}), f32[32,1,8]{2,1,0:T(1,128)S(1)}, u32[]{:S(2)}, u32[]{:S(2)}) async-start(f32[32,1,8]{2,1,0:T(1,128)} %bitcast.32), calls=%async_computation.2 | async-start | bytes 32768 | tf_op jit(solution)/shard_map/all_to_all | solution.py:58
Sparse Core Ops, SparseCore 0:
  63.9 6.2 sort.38.cloned.1.call-done
  73.4 4.3 sort.40.cloned.1.call-done
  (2 shorter events, 0.0 us)
